TPU v7x, 32 devices: a whole 2x2x4 slice. The times are simulated.
32 devices in a mesh: inp: 16 (over z, y, core), tm: 2 (over x).
Axes of the slice: x: 2, y: 2, z: 4, core: 2. Of those that a mesh axis runs over, the one named last changes fastest.
Arguments:
- samples: bfloat16 [512, 16384], P('inp', 'tm'), may hold values from -6 to 6
- tail: bfloat16 [512, 6144], P('inp'), may hold values from -6 to 6
- taps: float32 [4, 2048], replicated, may hold values from -3 to 3
- tile_table: int32 [16, 4], P('inp'), may hold values from 0 to 3, as said below
Outputs:
- visibilities: float32 [16, 4, 2, 32, 32, 1024], P('inp', None, None, None, None, 'tm')
Inputs may be any that keep to these rules, and one draw needn't show every extreme that they name: `tile_table`: each row holds 4 distinct offsets; offsets 0 and 3 both occur.
All inputs are finite; a program needn't handle non-finite values.
Results may differ from a plain program's by a relative error of at most 0.0064.
Values may be sent and summed in bfloat16 or wider, within the bound.
A program may use at most 128 MiB of HBM per device.

v0:
```python
import math
import jax
import jax.numpy as jnp
import numpy as np
from jax import lax
from jax.sharding import PartitionSpec as P

F = 1024
L = 2048
TAPS = 4
A_DEV = 32
S_DEV = 4
SPAN = 4


def shifted(array, axis, by):
    peers = lax.axis_size(axis)
    pairs = [(i, i + by) for i in range(peers) if 0 <= i + by < peers]
    return lax.ppermute(array, axis, pairs)


def shifted_2(block, axis, distance):
    devices = range(lax.axis_size(axis))
    route = [((i - distance) % len(devices), i) for i in devices]
    return lax.ppermute(block, axis, route)


def dft_basis():
    sample_rows = np.arange(L, dtype=np.int64)[:, None]
    channel_cols = np.arange(F, dtype=np.int64)[None, :]
    phase_index = sample_rows * channel_cols % L
    table_angles = np.arange(L, dtype=np.float32) * np.float32(2.0 * math.pi / L)
    norm_factor = np.float32(1.0 / math.sqrt(L))
    cosine_table = np.cos(table_angles).astype(np.float32) * norm_factor
    sine_table = -np.sin(table_angles).astype(np.float32) * norm_factor
    whole_table = np.concatenate([cosine_table[phase_index], sine_table[phase_index]], axis=1)
    return jnp.asarray(whole_table, dtype=jnp.bfloat16)


def channelize(frame_stack, count, taps, basis):
    filtered = taps[0][None, None, :] * frame_stack[:, 0:count, :].astype(jnp.float32)
    for tap in range(1, TAPS):
        filtered = filtered + taps[tap][None, None, :] * frame_stack[
            :, tap : tap + count, :
        ].astype(jnp.float32)
    filtered = filtered.astype(jnp.bfloat16).reshape(A_DEV * count, L)
    spectra = jnp.dot(filtered, basis, preferred_element_type=jnp.float32)
    return spectra.astype(jnp.bfloat16).reshape(A_DEV, count, 2, F)


def correlate_all(own_block, partners, spec_count):
    own_major = jnp.transpose(own_block, (3, 0, 2, 1))
    real_own = own_major[:, :, 0, :]
    imag_own = own_major[:, :, 1, :]
    upper_rows = jnp.concatenate([real_own, imag_own], axis=2)
    lower_rows = jnp.concatenate([imag_own, -real_own], axis=2)
    left_stack = jnp.concatenate([upper_rows, lower_rows], axis=1)
    tile_count = partners.shape[0]
    width = partners.shape[1]
    right_stack = jnp.transpose(partners, (4, 3, 2, 0, 1)).reshape(
        partners.shape[4], 2 * spec_count, tile_count * width
    )
    products = lax.dot_general(
        left_stack, right_stack, (((2,), (1,)), ((0,), (0,))), preferred_element_type=jnp.float32
    )
    products = products * (1.0 / spec_count)
    products = products.reshape(partners.shape[4], 2, width, tile_count, width)
    return jnp.transpose(products, (3, 1, 2, 4, 0))


def body(samples, tail, taps, tile_table):
    frames = samples.reshape(A_DEV, S_DEV, L)
    nearby = shifted(frames[:, : TAPS - 1, :], "tm", -1)
    at_end = lax.axis_index("tm") == lax.axis_size("tm") - 1
    trailing = jnp.where(at_end, tail.reshape(A_DEV, TAPS - 1, L), nearby)
    basis = dft_basis()
    complete = jnp.concatenate([frames, trailing], axis=1)
    spectra = channelize(complete, S_DEV, taps, basis)
    turned = lax.all_to_all(spectra, "tm", split_axis=3, concat_axis=1, tiled=True)
    spec_count = turned.shape[1]
    blocks = [turned]
    current = turned
    for section in range(1, SPAN):
        current = shifted_2(current, "inp", -1)
        blocks.append(current)
    holdings = jnp.stack(blocks, axis=0)
    partners = jnp.take(holdings, tile_table[0], axis=0)
    return correlate_all(turned, partners, spec_count)[None]


def solution(mesh):
    in_specs = (P("inp", "tm"), P("inp", None), P(), P("inp", None))
    out_specs = P("inp", None, None, None, None, "tm")
    return jax.shard_map(body, mesh=mesh, in_specs=in_specs, out_specs=out_specs, check_vma=False)
```

profile of v0, /device:TPU:0, one launch (start us, length us, event | category | flops | bytes accessed | tf_op | source)
XLA Modules:
  0.0 127.8 jit_solution(12264836127973082182)
XLA Ops:
  0.0 1.4 %reshape.57 = bf16[32,4,2048]{2,1,0:T(4,128)(2,1)S(1)} reshape(bf16[32,8192]{1,0:T(8,128)(2,1)} %param.5) | data formatting | bytes 1048576 | tf_op jit(solution)/shard_map/reshape | solution.py:72
  1.4 1.3 %collective-permute-start = (bf16[32,3,2048]{2,1,0:T(4,128)(2,1)S(1)}, bf16[32,3,2048]{2,1,0:T(4,128)(2,1)S(1)}, u32[]{:S(2)}, u32[]{:S(2)}) collective-permute-start(bf16[32,3,2048]{2,1,0:T(4,128)(2,1)S(1)} %bitcast.47), channel_id=1, source_target_pairs={{1,0},{3,2},{5,4},{7,6},{9,8},{11,10},{13,12},{15,14},{17,16},{19,... | collective-permute-start | bytes 1179656 | tf_op jit(solution)/shard_map/ppermute | solution.py:19
  2.7 1.7 %reshape.58 = bf16[32,3,2048]{2,1,0:T(4,128)(2,1)S(1)} reshape(bf16[32,6144]{1,0:T(8,128)(2,1)} %param.6) | data formatting | bytes 786432 | tf_op jit(solution)/shard_map/reshape | solution.py:75
  4.4 0.9 fusion.8
  5.4 12.3 %collective-permute-done = bf16[32,3,2048]{2,1,0:T(4,128)(2,1)S(1)} collective-permute-done((bf16[32,3,2048]{2,1,0:T(4,128)(2,1)S(1)}, bf16[32,3,2048]{2,1,0:T(4,128)(2,1)S(1)}, u32[]{:S(2)}, u32[]{:S(2)}) %collective-permute-start) | collective-permute-done | bytes 393248 | tf_op jit(solution)/shard_map/ppermute | solution.py:19
  17.6 0.3 broadcast_select_fusion.1
  17.9 1.8 %add_convert_fusion = bf16[32,4,2048]{2,1,0:T(4,128)(2,1)S(1)} fusion(bf16[32,4,2048]{2,1,0:T(4,128)(2,1)S(1)} %reshape.57, bf16[32,3,2048]{2,1,0:T(4,128)(2,1)S(1)} %broadcast_select_fusion.1, f32[2048]{0:T(1024)S(1)} %bitcast.51, f32[2048]{0:T(1024)S(1)} %bitcast.52, f32[2048]{0:T(1024)S(1)} %bitcast.50, f32[2048]{0:T(1024)S(1)} %bitcast.49), kind=kLoop, calls=%fused_computation.12 | loop fusion | flops 5505024 | bytes 1474560 | tf_op jit(solution)/shard_map/convert_element_type | solution.py:46
  19.8 0.1 reshape.59
  19.9 4.6 %convolution_convert_fusion = bf16[128,2048]{1,0:T(8,128)(2,1)S(1)} fusion(bf16[128,2048]{1,0:T(8,128)(2,1)S(1)} %reshape.59, bf16[2048,2048]{1,0:T(8,128)(2,1)} %constant.26.clone), kind=kOutput, calls=%fused_computation.2 | convolution fusion | flops 1074003968 | bytes 9437184 | tf_op jit(solution)/shard_map/dot_general | solution.py:47
  24.5 0.4 reshape.60
  24.9 1.7 %copy.30 = bf16[32,4,2,1024]{0,1,2,3:T(4,128)(2,1)S(1)} copy(bf16[32,4,2,1024]{3,2,1,0:T(2,128)(2,1)S(1)} %reshape.60) | data formatting | bytes 1048576 | tf_op jit(solution)/shard_map/reshape | solution.py:48
  26.6 2.1 %reshape.71 = bf16[2,2,65536]{2,1,0:T(2,128)(2,1)S(1)} reshape(bf16[1024,2,4,32]{3,2,1,0:T(4,128)(2,1)S(1)} %bitcast.42) | data formatting | bytes 1048576
  28.7 10.1 %all_to_all.18 = bf16[2,2,65536]{2,1,0:T(2,128)(2,1)S(1)} all-to-all(bf16[2,2,65536]{2,1,0:T(2,128)(2,1)S(1)} %reshape.71), channel_id=1, replica_groups=mesh['inp'=16,'tm'=2] {'tm'}, dimensions={0} | all-to-all | bytes 1048576 | tf_op jit(solution)/shard_map/all_to_all | solution.py:79
  38.8 1.0 reshape.72
  39.9 1.9 %copy.31 = bf16[32,2,4,2,512]{4,2,1,3,0:T(4,128)(2,1)S(1)} copy(bf16[32,2,4,2,512]{0,2,3,4,1:T(4,128)(2,1)S(1)} %bitcast.43) | data formatting | bytes 1048576 | tf_op jit(solution)/shard_map/all_to_all | solution.py:79
  41.8 0.1 all_to_all.16
  41.9 2.8 %collective-permute-start.1 = (bf16[32,8,2,512]{3,1,2,0:T(8,128)(2,1)S(1)}, bf16[32,8,2,512]{3,1,2,0:T(8,128)(2,1)S(1)}, u32[]{:S(2)}, u32[]{:S(2)}) collective-permute-start(bf16[32,8,2,512]{3,1,2,0:T(8,128)(2,1)S(1)} %all_to_all.16), channel_id=1, source_target_pairs={{2,0},{4,2},{6,4},{8,6},{10,8},{12,10},{14,12},{16,14},{18,16},{20... | collective-permute-start | bytes 1572872 | tf_op jit(solution)/shard_map/ppermute | solution.py:25
  44.7 6.7 %collective-permute-done.1 = bf16[32,8,2,512]{3,1,2,0:T(8,128)(2,1)S(1)} collective-permute-done((bf16[32,8,2,512]{3,1,2,0:T(8,128)(2,1)S(1)}, bf16[32,8,2,512]{3,1,2,0:T(8,128)(2,1)S(1)}, u32[]{:S(2)}, u32[]{:S(2)}) %collective-permute-start.1) | collective-permute-done | bytes 524320 | tf_op jit(solution)/shard_map/ppermute | solution.py:25
  51.4 4.6 %collective-permute-start.2 = (bf16[32,8,2,512]{3,1,2,0:T(8,128)(2,1)S(1)}, bf16[32,8,2,512]{3,1,2,0:T(8,128)(2,1)}, u32[]{:S(2)}, u32[]{:S(2)}) collective-permute-start(bf16[32,8,2,512]{3,1,2,0:T(8,128)(2,1)S(1)} %collective-permute-done.1), channel_id=1, source_target_pairs={{2,0},{4,2},{6,4},{8,6},{10,8},{12,10},{14,12},{16,14},{18,16},{20... | collective-permute-start | bytes 1572872 | tf_op jit(solution)/shard_map/ppermute | solution.py:25
  56.1 0.1 stack.15
  56.2 6.5 %collective-permute-done.2 = bf16[32,8,2,512]{3,1,2,0:T(8,128)(2,1)} collective-permute-done((bf16[32,8,2,512]{3,1,2,0:T(8,128)(2,1)S(1)}, bf16[32,8,2,512]{3,1,2,0:T(8,128)(2,1)}, u32[]{:S(2)}, u32[]{:S(2)}) %collective-permute-start.2) | collective-permute-done | bytes 524320 | tf_op jit(solution)/shard_map/ppermute | solution.py:25
  62.8 4.7 %collective-permute-start.3 = (bf16[32,8,2,512]{3,1,2,0:T(8,128)(2,1)}, bf16[32,8,2,512]{3,1,2,0:T(8,128)(2,1)}, u32[]{:S(2)}, u32[]{:S(2)}) collective-permute-start(bf16[32,8,2,512]{3,1,2,0:T(8,128)(2,1)} %collective-permute-done.2), channel_id=1, source_target_pairs={{2,0},{4,2},{6,4},{8,6},{10,8},{12,10},{14,12},{16,14},{18,16},{20... | collective-permute-start | bytes 1572872 | tf_op jit(solution)/shard_map/ppermute | solution.py:25
  67.7 3.0 %copy.32 = bf16[512,32,16]{1,2,0:T(8,128)(2,1)} copy(bf16[512,32,16]{0,2,1:T(8,128)(2,1)S(1)} %get-tuple-element.7) | data formatting | bytes 1048576 | tf_op jit(solution)/shard_map/concatenate | solution.py:55
  70.7 3.1 %copy.33 = bf16[512,32,16]{1,2,0:T(8,128)(2,1)} copy(bf16[512,32,16]{0,2,1:T(8,128)(2,1)S(1)} %get-tuple-element.8) | data formatting | bytes 1048576 | tf_op jit(solution)/shard_map/concatenate | solution.py:56
  73.8 0.7 collective-permute-done.3
  74.5 1.5 %pad_maximum_fusion = bf16[4,32,8,2,512]{4,2,3,1,0:T(8,128)(2,1)S(1)} fusion(bf16[1,32,8,2,512]{4,2,3,1,0:T(8,128)(2,1)} %bitcast.13, bf16[1,32,8,2,512]{4,2,3,1,0:T(8,128)(2,1)} %bitcast.12, bf16[1,32,8,2,512]{4,2,3,1,0:T(8,128)(2,1)S(1)} %bitcast.48, bf16[1,32,8,2,512]{4,2,3,1,0:T(8,128)(2,1)S(1)} %stack.15), kind=kLoop, calls=%fused_computation.6 | loop fusion | flops 3145728 | bytes 4194304 | tf_op jit(solution)/shard_map/stack | solution.py:86
  75.9 2.0 %gather_fusion = bf16[4,32,8,2,512]{4,2,3,1,0:T(8,128)(2,1)} fusion(bf16[4,32,8,2,512]{4,2,3,1,0:T(8,128)(2,1)S(1)} %pad_maximum_fusion, s32[1024]{0:T(1024)S(1)} %pad_clamp_fusion), kind=kCustom, calls=%fused_computation | custom fusion | bytes 4194320 | tf_op jit(solution)/shard_map/jit(_take)/gather | solution.py:87
  77.9 1.9 %broadcast_select_fusion = bf16[4,32,8,2,512]{4,2,3,1,0:T(8,128)(2,1)S(1)} fusion(bf16[4,32,8,2,512]{4,2,3,1,0:T(8,128)(2,1)} %gather_fusion, pred[4]{0:T(512)(128)(4,1)S(1)} %compare_and_fusion), kind=kLoop, calls=%fused_computation.7 | loop fusion | flops 1048576 | bytes 4194308 | tf_op jit(solution)/shard_map/jit(_take)/select_n | solution.py:87
  79.8 3.9 %copy.36 = bf16[512,16,128]{2,1,0:T(8,128)(2,1)} copy(bf16[512,16,128]{0,1,2:T(8,128)(2,1)S(1)} %bitcast.44) | data formatting | bytes 4194304 | tf_op jit(solution)/shard_map/reshape | solution.py:60
  83.7 14.2 %convolution_multiply_fusion = f32[512,64,128]{2,1,0:T(8,128)} fusion(bf16[512,16,128]{2,1,0:T(8,128)(2,1)} %copy.36, bf16[512,32,16]{1,2,0:T(8,128)(2,1)} %copy.33, bf16[512,32,16]{1,2,0:T(8,128)(2,1)} %copy.32), kind=kOutput, calls=%fused_computation.1 | convolution fusion | flops 140509184 | bytes 19922944 | tf_op jit(solution)/shard_map/dot_general | solution.py:63
  97.9 17.5 %copy.37 = f32[512,64,128]{0,2,1:T(8,128)} copy(f32[512,64,128]{2,1,0:T(8,128)} %convolution_multiply_fusion) | data formatting | bytes 33554432 | tf_op jit(solution)/shard_map/mul | solution.py:66
  115.4 12.4 %copy.38 = f32[1,4,2,32,32,512]{5,4,3,2,1,0:T(8,128)} copy(f32[1,4,2,32,32,512]{5,4,1,3,2,0:T(8,128)} %bitcast.41) | data formatting | bytes 33554432 | tf_op jit(solution)/shard_map/broadcast_in_dim | solution.py:88
  (12 shorter events, 0.2 us)
Async XLA Ops:
  1.4 16.2 %collective-permute-start = (bf16[32,3,2048]{2,1,0:T(4,128)(2,1)S(1)}, bf16[32,3,2048]{2,1,0:T(4,128)(2,1)S(1)}, u32[]{:S(2)}, u32[]{:S(2)}) collective-permute-start(bf16[32,3,2048]{2,1,0:T(4,128)(2,1)S(1)} %bitcast.47), channel_id=1, source_target_pairs={{1,0},{3,2},{5,4},{7,6},{9,8},{11,10},{13,12},{15,14},{17,16},{19,... | collective-permute-start | bytes 1179656 | tf_op jit(solution)/shard_map/ppermute | solution.py:19
  39.8 16.2 %copy-start.2 = (s32[1,4]{1,0:T(1,128)S(1)}, s32[1,4]{1,0:T(1,128)}, u32[]{:S(2)}) copy-start(s32[1,4]{1,0:T(1,128)} %param.8) | copy-start | bytes 52
  41.9 9.5 %collective-permute-start.1 = (bf16[32,8,2,512]{3,1,2,0:T(8,128)(2,1)S(1)}, bf16[32,8,2,512]{3,1,2,0:T(8,128)(2,1)S(1)}, u32[]{:S(2)}, u32[]{:S(2)}) collective-permute-start(bf16[32,8,2,512]{3,1,2,0:T(8,128)(2,1)S(1)} %all_to_all.16), channel_id=1, source_target_pairs={{2,0},{4,2},{6,4},{8,6},{10,8},{12,10},{14,12},{16,14},{18,16},{20... | collective-permute-start | bytes 1572872 | tf_op jit(solution)/shard_map/ppermute | solution.py:25
  51.4 16.1 %copy-start = (bf16[32,8,2,512]{3,1,2,0:T(8,128)(2,1)}, bf16[32,8,2,512]{3,1,2,0:T(8,128)(2,1)S(1)}, u32[]{:S(2)}) copy-start(bf16[32,8,2,512]{3,1,2,0:T(8,128)(2,1)S(1)} %collective-permute-done.1) | copy-start | bytes 1572868
  51.4 11.3 %collective-permute-start.2 = (bf16[32,8,2,512]{3,1,2,0:T(8,128)(2,1)S(1)}, bf16[32,8,2,512]{3,1,2,0:T(8,128)(2,1)}, u32[]{:S(2)}, u32[]{:S(2)}) collective-permute-start(bf16[32,8,2,512]{3,1,2,0:T(8,128)(2,1)S(1)} %collective-permute-done.1), channel_id=1, source_target_pairs={{2,0},{4,2},{6,4},{8,6},{10,8},{12,10},{14,12},{16,14},{18,16},{20... | collective-permute-start | bytes 1572872 | tf_op jit(solution)/shard_map/ppermute | solution.py:25
  62.8 11.7 %collective-permute-start.3 = (bf16[32,8,2,512]{3,1,2,0:T(8,128)(2,1)}, bf16[32,8,2,512]{3,1,2,0:T(8,128)(2,1)}, u32[]{:S(2)}, u32[]{:S(2)}) collective-permute-start(bf16[32,8,2,512]{3,1,2,0:T(8,128)(2,1)} %collective-permute-done.2), channel_id=1, source_target_pairs={{2,0},{4,2},{6,4},{8,6},{10,8},{12,10},{14,12},{16,14},{18,16},{20... | collective-permute-start | bytes 1572872 | tf_op jit(solution)/shard_map/ppermute | solution.py:25
  67.6 6.8 %copy-start.1 = (bf16[32,8,2,512]{3,1,2,0:T(8,128)(2,1)S(1)}, bf16[32,8,2,512]{3,1,2,0:T(8,128)(2,1)}, u32[]{:S(2)}) copy-start(bf16[32,8,2,512]{3,1,2,0:T(8,128)(2,1)} %copy-done) | copy-start | bytes 1572868
where the time goes:
time: 128 us
  local copies, waits for them, and re-layouts  53.4 us (42%)
  waiting for transfers between devices  26.3 us (21%)
  matrix products  18.8 us (15%)
  starting transfers between devices  13.4 us (10%)
  blocking collectives  10.1 us (8%)
  other arithmetic  5.56 us (4%)
    mul x1, local copies, waits for them, and re-layouts, correlate_all(): products = products * (1.0 / spec_count)  17.5 us
    dot_general x1, matrix products, correlate_all(): lax.dot_general(left_stack, right_stack, (((2,), (1,)), ((0,), (0,))), pr...  14.2 us
    ppermute x3, waiting for transfers between devices, shifted_2(): return lax.ppermute(block, axis, route)  14 us
    broadcast_in_dim x1, local copies, waits for them, and re-layouts, body(): return correlate_all(turned, partners, spec_count)[None]  12.4 us
    ppermute x1, waiting for transfers between devices, shifted(): return lax.ppermute(array, axis, pairs)  12.3 us
    ppermute x3, starting transfers between devices, shifted_2(): return lax.ppermute(block, axis, route)  12.1 us
    all_to_all x1, blocking collectives, body(): lax.all_to_all(spectra, 'tm', split_axis=3, concat_axis=1, tiled=True)  10.1 us
    dot_general x1, matrix products, channelize(): spectra = jnp.dot(filtered, basis, preferred_element_type=jnp.float32)  4.64 us
  transfers between devices with their start and end apart: 4, of which 4 were waited for; matrix products, arithmetic and copies ran while one was open for 7% of the time, Pallas kernels for 0%

commit v1 on v0

--- a/solution.py
+++ b/solution.py
@@ -1,9 +1,11 @@
+import functools
 import math
 import jax
 import jax.numpy as jnp
 import numpy as np
 from jax import lax
 from jax.sharding import PartitionSpec as P
+from jax.lax import all_to_all, axis_size
 
 F = 1024
 L = 2048
@@ -11,6 +13,19 @@
 A_DEV = 32
 S_DEV = 4
 SPAN = 4
+
+
+def _do_rows(u_in, mesh_dim):
+    passed = all_to_all(
+        jnp.stack(jnp.split(u_in, axis_size(mesh_dim), axis=3)),
+        axis_name=mesh_dim,
+        split_axis=0,
+        concat_axis=0,
+    )
+    return jnp.concatenate(passed, axis=1)
+
+
+start_the_page = functools.partial(_do_rows, mesh_dim="tm")
 
 
 def shifted(array, axis, by):
@@ -76,7 +91,7 @@
     basis = dft_basis()
     complete = jnp.concatenate([frames, trailing], axis=1)
     spectra = channelize(complete, S_DEV, taps, basis)
-    turned = lax.all_to_all(spectra, "tm", split_axis=3, concat_axis=1, tiled=True)
+    turned = start_the_page(spectra)
     spec_count = turned.shape[1]
     blocks = [turned]
     current = turned

time: 128 us -> 123 us (0.961)
  local copies, waits for them, and re-layouts: 53.4 us -> 47.4 us
    unnamed x8 -> x2, local copies, waits for them, and re-layouts: 3.11 us -> 0.01 us
    all_to_all x2 -> x0, local copies, waits for them, and re-layouts: 2.06 us -> none  [body(): lax.all_to_all(spectra, 'tm', split_axis=3, concat_axis=1, tiled=True)]
    reshape x2 -> x1, local copies, waits for them, and re-layouts: 2.04 us -> 0.38 us  [channelize(): return spectra.astype(jnp.bfloat16).reshape(A_DEV, count, 2, F)]
where the time goes in v1:
time: 123 us; the launch traced here: 122 us
  local copies, waits for them, and re-layouts  47.4 us (39%)
  waiting for transfers between devices  26.3 us (21%)
  matrix products  18.8 us (15%)
  starting transfers between devices  13.4 us (11%)
  blocking collectives  10.1 us (8%)
  other arithmetic  6.29 us (5%)
    mul x1, local copies, waits for them, and re-layouts, correlate_all(): products = products * (1.0 / spec_count)  17.5 us
    dot_general x1, matrix products, correlate_all(): lax.dot_general(left_stack, right_stack, (((2,), (1,)), ((0,), (0,))), pr...  14.2 us
    ppermute x3, waiting for transfers between devices, shifted_2(): return lax.ppermute(block, axis, route)  14 us
    broadcast_in_dim x1, local copies, waits for them, and re-layouts, body(): return correlate_all(turned, partners, spec_count)[None]  12.4 us
    ppermute x1, waiting for transfers between devices, shifted(): return lax.ppermute(array, axis, pairs)  12.3 us
    ppermute x3, starting transfers between devices, shifted_2(): return lax.ppermute(block, axis, route)  12.1 us
    all_to_all x1, blocking collectives, _do_rows(): all_to_all(jnp.stack(jnp.split(u_in, axis_size(mesh_dim), axis=3)), axis_...  10.1 us
    dot_general x1, matrix products, channelize(): spectra = jnp.dot(filtered, basis, preferred_element_type=jnp.float32)  4.64 us
  transfers between devices with their start and end apart: 4, of which 4 were waited for; matrix products, arithmetic and copies ran while one was open for 7% of the time, Pallas kernels for 0%

profile of v1, /device:TPU:0, one launch (start us, length us, event | category | flops | bytes accessed | tf_op | source)
XLA Modules:
  0.0 122.5 jit_solution(17000344314586371005)
XLA Ops:
  0.0 1.4 %reshape.62 = bf16[32,4,2048]{2,1,0:T(4,128)(2,1)S(1)} reshape(bf16[32,8192]{1,0:T(8,128)(2,1)} %param.5) | data formatting | bytes 1048576 | tf_op jit(solution)/shard_map/reshape | solution.py:87
  1.4 1.3 %collective-permute-start = (bf16[32,3,2048]{2,1,0:T(4,128)(2,1)S(1)}, bf16[32,3,2048]{2,1,0:T(4,128)(2,1)S(1)}, u32[]{:S(2)}, u32[]{:S(2)}) collective-permute-start(bf16[32,3,2048]{2,1,0:T(4,128)(2,1)S(1)} %bitcast.45), channel_id=1, source_target_pairs={{1,0},{3,2},{5,4},{7,6},{9,8},{11,10},{13,12},{15,14},{17,16},{19,... | collective-permute-start | bytes 1179656 | tf_op jit(solution)/shard_map/ppermute | solution.py:34
  2.7 1.7 %reshape.63 = bf16[32,3,2048]{2,1,0:T(4,128)(2,1)S(1)} reshape(bf16[32,6144]{1,0:T(8,128)(2,1)} %param.6) | data formatting | bytes 786432 | tf_op jit(solution)/shard_map/reshape | solution.py:90
  4.4 0.9 fusion.8
  5.4 12.3 %collective-permute-done = bf16[32,3,2048]{2,1,0:T(4,128)(2,1)S(1)} collective-permute-done((bf16[32,3,2048]{2,1,0:T(4,128)(2,1)S(1)}, bf16[32,3,2048]{2,1,0:T(4,128)(2,1)S(1)}, u32[]{:S(2)}, u32[]{:S(2)}) %collective-permute-start) | collective-permute-done | bytes 393248 | tf_op jit(solution)/shard_map/ppermute | solution.py:34
  17.6 0.3 broadcast_select_fusion.1
  17.9 1.8 %add_convert_fusion = bf16[32,4,2048]{2,1,0:T(4,128)(2,1)S(1)} fusion(bf16[32,4,2048]{2,1,0:T(4,128)(2,1)S(1)} %reshape.62, bf16[32,3,2048]{2,1,0:T(4,128)(2,1)S(1)} %broadcast_select_fusion.1, f32[2048]{0:T(1024)S(1)} %bitcast.50, f32[2048]{0:T(1024)S(1)} %bitcast.51, f32[2048]{0:T(1024)S(1)} %bitcast.49, f32[2048]{0:T(1024)S(1)} %bitcast.48), kind=kLoop, calls=%fused_computation.12 | loop fusion | flops 5505024 | bytes 1474560 | tf_op jit(solution)/shard_map/convert_element_type | solution.py:61
  19.8 0.1 reshape.64
  19.9 4.6 %convolution_convert_fusion = bf16[128,2048]{1,0:T(8,128)(2,1)S(1)} fusion(bf16[128,2048]{1,0:T(8,128)(2,1)S(1)} %reshape.64, bf16[2048,2048]{1,0:T(8,128)(2,1)} %constant.26.clone), kind=kOutput, calls=%fused_computation.2 | convolution fusion | flops 1074003968 | bytes 9437184 | tf_op jit(solution)/shard_map/dot_general | solution.py:62
  24.5 0.4 reshape.65
  24.9 0.4 slice_bitcast_fusion.3
  25.3 0.7 pad_maximum_fusion.2
  26.0 10.1 %all_to_all.5 = bf16[2,32,4,2,512]{4,3,2,1,0:T(2,128)(2,1)S(1)} all-to-all(bf16[2,32,4,2,512]{4,3,2,1,0:T(2,128)(2,1)S(1)} %pad_maximum_fusion.2), channel_id=1, replica_groups=mesh['inp'=16,'tm'=2] {'tm'}, dimensions={0} | all-to-all | bytes 1048576 | tf_op jit(solution)/shard_map/all_to_all | solution.py:19
  36.2 0.3 copy.22
  36.5 0.1 reshape.67
  36.6 2.8 %collective-permute-start.1 = (bf16[32,8,2,512]{3,1,2,0:T(8,128)(2,1)S(1)}, bf16[32,8,2,512]{3,1,2,0:T(8,128)(2,1)S(1)}, u32[]{:S(2)}, u32[]{:S(2)}) collective-permute-start(bf16[32,8,2,512]{3,1,2,0:T(8,128)(2,1)S(1)} %reshape.67), channel_id=1, source_target_pairs={{2,0},{4,2},{6,4},{8,6},{10,8},{12,10},{14,12},{16,14},{18,16},{20... | collective-permute-start | bytes 1572872 | tf_op jit(solution)/shard_map/ppermute | solution.py:40
  39.4 6.7 %collective-permute-done.1 = bf16[32,8,2,512]{3,1,2,0:T(8,128)(2,1)S(1)} collective-permute-done((bf16[32,8,2,512]{3,1,2,0:T(8,128)(2,1)S(1)}, bf16[32,8,2,512]{3,1,2,0:T(8,128)(2,1)S(1)}, u32[]{:S(2)}, u32[]{:S(2)}) %collective-permute-start.1) | collective-permute-done | bytes 524320 | tf_op jit(solution)/shard_map/ppermute | solution.py:40
  46.1 4.6 %collective-permute-start.2 = (bf16[32,8,2,512]{3,1,2,0:T(8,128)(2,1)S(1)}, bf16[32,8,2,512]{3,1,2,0:T(8,128)(2,1)}, u32[]{:S(2)}, u32[]{:S(2)}) collective-permute-start(bf16[32,8,2,512]{3,1,2,0:T(8,128)(2,1)S(1)} %collective-permute-done.1), channel_id=1, source_target_pairs={{2,0},{4,2},{6,4},{8,6},{10,8},{12,10},{14,12},{16,14},{18,16},{20... | collective-permute-start | bytes 1572872 | tf_op jit(solution)/shard_map/ppermute | solution.py:40
  50.8 0.1 stack_reshape.3
  50.9 6.5 %collective-permute-done.2 = bf16[32,8,2,512]{3,1,2,0:T(8,128)(2,1)} collective-permute-done((bf16[32,8,2,512]{3,1,2,0:T(8,128)(2,1)S(1)}, bf16[32,8,2,512]{3,1,2,0:T(8,128)(2,1)}, u32[]{:S(2)}, u32[]{:S(2)}) %collective-permute-start.2) | collective-permute-done | bytes 524320 | tf_op jit(solution)/shard_map/ppermute | solution.py:40
  57.4 4.7 %collective-permute-start.3 = (bf16[32,8,2,512]{3,1,2,0:T(8,128)(2,1)}, bf16[32,8,2,512]{3,1,2,0:T(8,128)(2,1)}, u32[]{:S(2)}, u32[]{:S(2)}) collective-permute-start(bf16[32,8,2,512]{3,1,2,0:T(8,128)(2,1)} %collective-permute-done.2), channel_id=1, source_target_pairs={{2,0},{4,2},{6,4},{8,6},{10,8},{12,10},{14,12},{16,14},{18,16},{20... | collective-permute-start | bytes 1572872 | tf_op jit(solution)/shard_map/ppermute | solution.py:40
  62.2 0.1 pad_maximum_fusion.3
  62.3 3.0 %copy.23 = bf16[512,32,16]{1,2,0:T(8,128)(2,1)} copy(bf16[512,32,16]{0,2,1:T(8,128)(2,1)S(1)} %get-tuple-element.9) | data formatting | bytes 1048576 | tf_op jit(solution)/shard_map/concatenate | solution.py:70
  65.3 3.1 %copy.24 = bf16[512,32,16]{1,2,0:T(8,128)(2,1)} copy(bf16[512,32,16]{0,2,1:T(8,128)(2,1)S(1)} %get-tuple-element.10) | data formatting | bytes 1048576 | tf_op jit(solution)/shard_map/concatenate | solution.py:71
  68.4 0.8 collective-permute-done.3
  69.2 1.5 %pad_maximum_fusion = bf16[4,32,8,2,512]{4,2,3,1,0:T(8,128)(2,1)S(1)} fusion(bf16[1,32,8,2,512]{4,2,3,1,0:T(8,128)(2,1)} %bitcast.13, bf16[1,32,8,2,512]{4,2,3,1,0:T(8,128)(2,1)} %bitcast.12, bf16[1,32,8,2,512]{4,2,3,1,0:T(8,128)(2,1)S(1)} %bitcast.47, bf16[1,32,8,2,512]{4,2,3,1,0:T(8,128)(2,1)S(1)} %stack_reshape.3), kind=kLoop, calls=%fused_computation.6 | loop fusion | flops 3145728 | bytes 4194304 | tf_op jit(solution)/shard_map/stack | solution.py:101
  70.6 2.0 %gather_fusion = bf16[4,32,8,2,512]{4,2,3,1,0:T(8,128)(2,1)} fusion(bf16[4,32,8,2,512]{4,2,3,1,0:T(8,128)(2,1)S(1)} %pad_maximum_fusion, s32[1024]{0:T(1024)S(1)} %pad_clamp_fusion), kind=kCustom, calls=%fused_computation | custom fusion | bytes 4194320 | tf_op jit(solution)/shard_map/jit(_take)/gather | solution.py:102
  72.6 1.9 %broadcast_select_fusion = bf16[4,32,8,2,512]{4,2,3,1,0:T(8,128)(2,1)S(1)} fusion(bf16[4,32,8,2,512]{4,2,3,1,0:T(8,128)(2,1)} %gather_fusion, pred[4]{0:T(512)(128)(4,1)S(1)} %compare_and_fusion), kind=kLoop, calls=%fused_computation.7 | loop fusion | flops 1048576 | bytes 4194308 | tf_op jit(solution)/shard_map/jit(_take)/select_n | solution.py:102
  74.5 3.9 %copy.27 = bf16[512,16,128]{2,1,0:T(8,128)(2,1)} copy(bf16[512,16,128]{0,1,2:T(8,128)(2,1)S(1)} %bitcast.42) | data formatting | bytes 4194304 | tf_op jit(solution)/shard_map/reshape | solution.py:75
  78.4 14.2 %convolution_multiply_fusion = f32[512,64,128]{2,1,0:T(8,128)} fusion(bf16[512,16,128]{2,1,0:T(8,128)(2,1)} %copy.27, bf16[512,32,16]{1,2,0:T(8,128)(2,1)} %copy.24, bf16[512,32,16]{1,2,0:T(8,128)(2,1)} %copy.23), kind=kOutput, calls=%fused_computation.1 | convolution fusion | flops 140509184 | bytes 19922944 | tf_op jit(solution)/shard_map/dot_general | solution.py:78
  92.6 17.5 %copy.28 = f32[512,64,128]{0,2,1:T(8,128)} copy(f32[512,64,128]{2,1,0:T(8,128)} %convolution_multiply_fusion) | data formatting | bytes 33554432 | tf_op jit(solution)/shard_map/mul | solution.py:81
  110.1 12.4 %copy.29 = f32[1,4,2,32,32,512]{5,4,3,2,1,0:T(8,128)} copy(f32[1,4,2,32,32,512]{5,4,1,3,2,0:T(8,128)} %bitcast.41) | data formatting | bytes 33554432 | tf_op jit(solution)/shard_map/broadcast_in_dim | solution.py:103
  (7 shorter events, 0.1 us)
Async XLA Ops:
  1.4 16.2 %collective-permute-start = (bf16[32,3,2048]{2,1,0:T(4,128)(2,1)S(1)}, bf16[32,3,2048]{2,1,0:T(4,128)(2,1)S(1)}, u32[]{:S(2)}, u32[]{:S(2)}) collective-permute-start(bf16[32,3,2048]{2,1,0:T(4,128)(2,1)S(1)} %bitcast.45), channel_id=1, source_target_pairs={{1,0},{3,2},{5,4},{7,6},{9,8},{11,10},{13,12},{15,14},{17,16},{19,... | collective-permute-start | bytes 1179656 | tf_op jit(solution)/shard_map/ppermute | solution.py:34
  25.3 25.4 %copy-start = (s32[1,4]{1,0:T(1,128)S(1)}, s32[1,4]{1,0:T(1,128)}, u32[]{:S(2)}) copy-start(s32[1,4]{1,0:T(1,128)} %param.8) | copy-start | bytes 52
  36.6 9.5 %collective-permute-start.1 = (bf16[32,8,2,512]{3,1,2,0:T(8,128)(2,1)S(1)}, bf16[32,8,2,512]{3,1,2,0:T(8,128)(2,1)S(1)}, u32[]{:S(2)}, u32[]{:S(2)}) collective-permute-start(bf16[32,8,2,512]{3,1,2,0:T(8,128)(2,1)S(1)} %reshape.67), channel_id=1, source_target_pairs={{2,0},{4,2},{6,4},{8,6},{10,8},{12,10},{14,12},{16,14},{18,16},{20... | collective-permute-start | bytes 1572872 | tf_op jit(solution)/shard_map/ppermute | solution.py:40
  46.1 11.3 %collective-permute-start.2 = (bf16[32,8,2,512]{3,1,2,0:T(8,128)(2,1)S(1)}, bf16[32,8,2,512]{3,1,2,0:T(8,128)(2,1)}, u32[]{:S(2)}, u32[]{:S(2)}) collective-permute-start(bf16[32,8,2,512]{3,1,2,0:T(8,128)(2,1)S(1)} %collective-permute-done.1), channel_id=1, source_target_pairs={{2,0},{4,2},{6,4},{8,6},{10,8},{12,10},{14,12},{16,14},{18,16},{20... | collective-permute-start | bytes 1572872 | tf_op jit(solution)/shard_map/ppermute | solution.py:40
  57.4 11.7 %collective-permute-start.3 = (bf16[32,8,2,512]{3,1,2,0:T(8,128)(2,1)}, bf16[32,8,2,512]{3,1,2,0:T(8,128)(2,1)}, u32[]{:S(2)}, u32[]{:S(2)}) collective-permute-start(bf16[32,8,2,512]{3,1,2,0:T(8,128)(2,1)} %collective-permute-done.2), channel_id=1, source_target_pairs={{2,0},{4,2},{6,4},{8,6},{10,8},{12,10},{14,12},{16,14},{18,16},{20... | collective-permute-start | bytes 1572872 | tf_op jit(solution)/shard_map/ppermute | solution.py:40
